TPU v7x, 32 devices: a whole 2x2x4 slice. The times are simulated.
32 devices in a mesh: comp: 2 (over y), gx: 8 (over z, core), gy: 2 (over x).
Axes of the slice: x: 2, y: 2, z: 4, core: 2. Of those that a mesh axis runs over, the one named last changes fastest.
Arguments:
- state: float32 [2, 7, 256, 64, 128], P('comp', None, 'gx', 'gy'), may hold values from -6 to 6
- diffusivity: float32 [2, 7], replicated, may hold values from 0.01 to 0.06
- advection: float32 [2, 7], replicated, may hold values from 0.05 to 0.3
- solid_mask: int32 [256, 64, 128], P('gx', 'gy'), may hold values 0 or 1
- iface_map: int32 [64], P('gy'), may hold values from 0 to 63, each once
Outputs:
- new_state: float32 [2, 7, 256, 64, 128], P('comp', None, 'gx', 'gy')
Inputs may be any that keep to these rules, and one draw needn't show every extreme that they name: `iface_map`: each turbine inlet row takes exactly one combustor exit-plane row, and every exit-plane row is taken once.
All inputs are finite; a program needn't handle non-finite values. No bound on the sum of `solid_mask` on one device may be relied on, other than what follows from the above.
Results may differ from a plain program's by a relative error of at most 0.0014.
Values may be sent and summed in bfloat16 or wider, within the bound.
No kernel may reach another device: no remote copies, remote signals or barrier semaphores. Data moves between devices by JAX's collectives and lax.ppermute only.
A program may use at most 64 MiB of HBM per device.

v0:
```python
import jax
import jax.numpy as jnp
from jax import lax
from jax.sharding import PartitionSpec as P

RATIO = 1.5
GAIN = 0.4


def swapped(block, axis, apart):
    count = lax.axis_size(axis)
    route = []
    for low in range(count):
        high = low | 1 << apart
        if high != low and high < count:
            route += [(low, high), (high, low)]
    return lax.ppermute(block, axis, route)


def extended(block, sides, width):
    for axis, dim in sides:
        count = lax.axis_size(axis)
        forward = [(i, i + 1) for i in range(count - 1)]
        forward.append((count - 1, 0))
        backward = [(target, source) for source, target in forward]
        low = lax.ppermute(
            lax.slice_in_dim(block, block.shape[dim] - width, None, axis=dim), axis, forward
        )
        high = lax.ppermute(lax.slice_in_dim(block, 0, width, axis=dim), axis, backward)
        block = jnp.concatenate([low, block, high], axis=dim)
    return block


def rates(padded, solid, diff, speed):
    gfac = jnp.exp(GAIN * jnp.tanh(padded[4]))[None]
    mid = padded[:, 1:-1, 1:-1]
    east = padded[:, 2:, 1:-1]
    west = padded[:, :-2, 1:-1]
    north = padded[:, 1:-1, 2:]
    south = padded[:, 1:-1, :-2]
    gmid = gfac[:, 1:-1, 1:-1]
    geast = gfac[:, 2:, 1:-1]
    gwest = gfac[:, :-2, 1:-1]
    gnorth = gfac[:, 1:-1, 2:]
    gsouth = gfac[:, 1:-1, :-2]
    upper = jnp.roll(mid, -1, 3)
    lower = jnp.roll(mid, 1, 3)
    gupper = jnp.roll(gmid, -1, 3)
    glower = jnp.roll(gmid, 1, 3)
    along_x = 0.5 * (gmid + geast) * (east - mid) - 0.5 * (gmid + gwest) * (mid - west)
    along_y = 0.5 * (gmid + gnorth) * (north - mid) - 0.5 * (gmid + gsouth) * (mid - south)
    along_z = 0.5 * (gmid + gupper) * (upper - mid) - 0.5 * (gmid + glower) * (mid - lower)
    diffusion = along_x + along_y + along_z
    dcol = diff[:, None, None, None]
    scol = speed[:, None, None, None]
    fluid = dcol * diffusion - scol * (0.5 * (east - west))
    return jnp.where(solid[None], RATIO * dcol * diffusion, fluid)


def set_edges(padded, first_row, last_row, left_value, on_left, on_right):
    padded = padded.at[:, first_row].set(jnp.where(on_left, left_value, padded[:, first_row]))
    return padded.at[:, last_row].set(
        jnp.where(on_right, jnp.zeros_like(left_value), padded[:, last_row])
    )


def edge_rows(interface, map_whole, row_ids, turbine):
    inflow = jnp.take(interface, jnp.take(map_whole, row_ids), axis=1)
    matches = map_whole[None, :] == row_ids[:, None]
    counting = jnp.arange(map_whole.shape[0], dtype=jnp.int32)[None, :]
    anchor = jnp.sum(jnp.where(matches, counting, 0), axis=1)
    backflow = jnp.take(interface, anchor, axis=1)
    return jnp.where(turbine, inflow, backflow)


def body(state, diffusivity, advection, solid_mask, iface_map):
    fields = state[0]
    comp_pos = lax.axis_index("comp")
    turbine = comp_pos == 1
    diff = lax.dynamic_index_in_dim(diffusivity, comp_pos, 0, keepdims=False)
    speed_raw = lax.dynamic_index_in_dim(advection, comp_pos, 0, keepdims=False)
    speed = jnp.where(turbine, speed_raw, -speed_raw)
    stream_pos = lax.axis_index("gx")
    last_block = lax.axis_size("gx") - 1
    on_left = stream_pos == 0
    on_right = stream_pos == last_block
    solid = (solid_mask == 1) & turbine
    across = swapped(fields[:, 0].astype(jnp.bfloat16), "comp", 0).astype(jnp.float32)
    interface = lax.all_gather(across.astype(jnp.bfloat16), "gy", axis=1, tiled=True).astype(
        across.dtype
    )
    map_whole = lax.all_gather(iface_map, "gy", axis=0, tiled=True)
    rows_dev = fields.shape[2]
    row_base = lax.axis_index("gy") * rows_dev
    row_ids = row_base + jnp.arange(rows_dev, dtype=jnp.int32)
    left_value = edge_rows(interface, map_whole, row_ids, turbine)
    left_full = jnp.pad(left_value, ((0, 0), (1, 1), (0, 0)))

    def with_rim(block):
        padded = extended(block.astype(jnp.bfloat16), (("gx", 1), ("gy", 2)), 1).astype(block.dtype)
        return set_edges(padded, 0, -1, left_full, on_left, on_right)

    first = fields + rates(with_rim(fields), solid, diff, speed)
    second = rates(with_rim(first), solid, diff, speed)
    result = 0.5 * fields + 0.5 * (first + second)
    return result[None]


def solution(mesh):
    return jax.shard_map(
        body,
        mesh=mesh,
        in_specs=(P("comp", None, "gx", "gy", None), P(), P(), P("gx", "gy", None), P("gy")),
        out_specs=P("comp", None, "gx", "gy", None),
        check_vma=False,
    )
```

profile of v0, /device:TPU:0, one launch (start us, length us, event | category | flops | bytes accessed | tf_op | source)
XLA Modules:
  0.0 103.4 jit_solution(14877481706035770598)
XLA Ops:
  0.0 5.4 %copy.31 = bf16[1,7,32,32,128]{4,1,3,2,0:T(8,128)(2,1)S(1)} copy(f32[1,7,32,32,128]{4,3,2,1,0:T(8,128)} %param.15) | data formatting | bytes 5505024 | tf_op args[0]
  5.4 3.0 %collective-permute-start.4 = (bf16[7,32,128]{2,0,1:T(8,128)(2,1)S(1)}, bf16[7,32,128]{2,0,1:T(8,128)(2,1)S(1)}, u32[]{:S(2)}, u32[]{:S(2)}) collective-permute-start(bf16[7,32,128]{2,0,1:T(8,128)(2,1)S(1)} %get-tuple-element.74), channel_id=1, source_target_pairs={{0,16},{16,0},{1,17},{17,1},{2,18},{18,2},{3,19},{19,3},{4,20},{20... | collective-permute-start | bytes 172040 | tf_op jit(solution)/shard_map/ppermute | solution.py:17
  8.5 2.8 %collective-permute-start.1 = (bf16[7,1,32,128]{3,0,2,1:T(8,128)(2,1)S(1)}, bf16[7,1,32,128]{3,0,2,1:T(8,128)(2,1)S(1)}, u32[]{:S(2)}, u32[]{:S(2)}) collective-permute-start(bf16[7,1,32,128]{3,0,2,1:T(8,128)(2,1)S(1)} %get-tuple-element.75), channel_id=1, source_target_pairs={{2,0},{4,2},{6,4},{8,6},{10,8},{12,10},{14,12},{0,14},{3,1},{5,3},... | collective-permute-start | bytes 172040 | tf_op jit(solution)/shard_map/ppermute | solution.py:29
  12.8 4.3 %all-reduce.1 = s32[64]{0:T(128)S(1)} all-reduce(s32[64]{0:T(128)S(1)} %dynamic-update-slice.12), channel_id=1, replica_groups=mesh['comp'=2,'gx'=8,'gy'=2] {'gy'}, use_global_device_ids=true, to_apply=%add.1 | all-reduce | flops 64 | bytes 512
  18.2 5.6 %all_gather.6 = bf16[7,64,128]{2,1,0:T(8,128)(2,1)S(1)} all-gather(bf16[7,32,128]{2,1,0:T(8,128)(2,1)S(1)} %copy.19), channel_id=1, replica_groups=mesh['comp'=2,'gx'=8,'gy'=2] {'gy'}, dimensions={1}, use_global_device_ids=true | all-gather | bytes 172032 | tf_op jit(solution)/shard_map/all_gather | solution.py:89
  23.9 1.6 %collective-permute-start.2 = (bf16[7,34,1,128]{3,0,2,1:T(8,128)(2,1)S(1)}, bf16[7,34,1,128]{3,0,2,1:T(8,128)(2,1)S(1)}, u32[]{:S(2)}, u32[]{:S(2)}) collective-permute-start(bf16[7,34,1,128]{3,0,2,1:T(8,128)(2,1)S(1)} %get-tuple-element.70), channel_id=1, source_target_pairs={{0,1},{1,0},{2,3},{3,2},{4,5},{5,4},{6,7},{7,6},{8,9},{9,8},{10,11... | collective-permute-start | bytes 182792 | tf_op jit(solution)/shard_map/ppermute | solution.py:26
  28.3 1.5 %collective-permute-done.3 = bf16[7,34,1,128]{3,0,2,1:T(8,128)(2,1)S(1)} collective-permute-done((bf16[7,34,1,128]{3,0,2,1:T(8,128)(2,1)S(1)}, bf16[7,34,1,128]{3,0,2,1:T(8,128)(2,1)S(1)}, u32[]{:S(2)}, u32[]{:S(2)}) %collective-permute-start.3) | collective-permute-done | bytes 60960 | tf_op jit(solution)/shard_map/ppermute | solution.py:29
  29.8 1.3 %maximum_convert_fusion = f32[7,34,34,128]{3,0,2,1:T(8,128)S(1)} fusion(bf16[7,34,1,128]{3,0,2,1:T(8,128)(2,1)S(1)} %collective-permute-done.3, bf16[7,1,32,128]{3,0,2,1:T(8,128)(2,1)S(1)} %collective-permute-done.1, bf16[7,32,32,128]{3,0,2,1:T(8,128)(2,1)S(1)} %bitcast.66, bf16[7,1,32,128]{3,0,2,1:T(8,128)(2,1)S(1)} %collective-permute-done, ...), kind=kLoop, calls=%fused_computation.32 | loop fusion | flops 5178880 | bytes 6214656 | tf_op jit(solution)/shard_map/convert_element_type | solution.py:100
  31.2 1.2 %fusion.21 = f32[1,34,34,128]{3,0,2,1:T(1,128)S(1)} fusion(f32[7,34,34,128]{3,0,2,1:T(8,128)S(1)} %fusion.38), kind=kLoop, calls=%fused_computation.39 | loop fusion | flops 147968 | bytes 1183744 | tf_op jit(solution)/shard_map/exp | solution.py:35
  34.7 3.5 %fusion.51 = (f32[7,32,32,1]{3,0,2,1:T(8,128)S(1)}, f32[7,32,32,1]{3,0,2,1:T(8,128)}) fusion(f32[7,34,34,128]{3,0,2,1:T(8,128)S(1)} %fusion.38), kind=kLoop, calls=%fused_computation.110 | loop fusion | bytes 114688 | tf_op jit(solution)/shard_map/jit(_roll_static)/slice | solution.py:46
  38.2 4.8 %fusion.50 = (f32[7,32,32,127]{3,0,2,1:T(8,128)}, f32[7,32,32,127]{3,0,2,1:T(8,128)}) fusion(f32[7,34,34,128]{3,0,2,1:T(8,128)S(1)} %fusion.38), kind=kLoop, calls=%fused_computation.109 | loop fusion | bytes 14565376 | tf_op jit(solution)/shard_map/jit(_roll_static)/slice | solution.py:46
  43.1 4.4 %fusion.29 = (f32[1,32,32,128]{3,0,2,1:T(1,128)S(1)}, f32[1,32,32,128]{3,0,2,1:T(1,128)S(1)}, f32[1,32,32,128]{3,0,2,1:T(1,128)S(1)}, f32[1,32,32,128]{3,0,2,1:T...) fusion(f32[1,34,34,128]{3,0,2,1:T(1,128)S(1)} %fusion.21, ...), kind=kLoop, calls=%fused_computation.55 | loop fusion | flops 1835008 | bytes 6815744 | tf_op jit(solution)/shard_map/mul | solution.py:50
  47.5 11.8 %fusion.46 = (bf16[7,32,32,128]{3,0,2,1:T(8,128)(2,1)S(1)}, f32[7,32,32,128]{3,0,2,1:T(8,128)S(1)}) fusion(f32[7]{0:T(128)S(1)} %fusion.42, f32[7]{0:T(128)S(1)} %get-tuple-element.57, f32[7,32,32,127]{3,0,2,1:T(8,128)} %get-tuple-element.65, f32[7,32,32,1]{3,0,2,1:T(8,128)} %get-tuple-element.67, f32[32,32,128]{2,1,0:T(8,128)S(1)} %bitcast.74, ...), kind=kLoop, calls=%fused_computation.106 | loop fusion | flops 24772608 | bytes 38142036 | tf_op jit(solution)/shard_map/convert_element_type | solution.py:100
  59.4 3.5 %collective-permute-start.6 = (bf16[7,1,32,128]{3,0,2,1:T(8,128)(2,1)S(1)}, bf16[7,1,32,128]{3,0,2,1:T(8,128)(2,1)S(1)}, u32[]{:S(2)}, u32[]{:S(2)}) collective-permute-start(bf16[7,1,32,128]{3,0,2,1:T(8,128)(2,1)S(1)} %get-tuple-element.73), channel_id=1, source_target_pairs={{2,0},{4,2},{6,4},{8,6},{10,8},{12,10},{14,12},{0,14},{3,1},{5,3},... | collective-permute-start | bytes 172040 | tf_op jit(solution)/shard_map/ppermute | solution.py:29
  62.9 2.1 %collective-permute-done.5 = bf16[7,1,32,128]{3,0,2,1:T(8,128)(2,1)S(1)} collective-permute-done((bf16[7,1,32,128]{3,0,2,1:T(8,128)(2,1)S(1)}, bf16[7,1,32,128]{3,0,2,1:T(8,128)(2,1)S(1)}, u32[]{:S(2)}, u32[]{:S(2)}) %collective-permute-start.5) | collective-permute-done | bytes 57376 | tf_op jit(solution)/shard_map/ppermute | solution.py:26
  65.1 1.2 %collective-permute-start.7 = (bf16[7,34,1,128]{3,0,2,1:T(8,128)(2,1)S(1)}, bf16[7,34,1,128]{3,0,2,1:T(8,128)(2,1)S(1)}, u32[]{:S(2)}, u32[]{:S(2)}) collective-permute-start(bf16[7,34,1,128]{3,0,2,1:T(8,128)(2,1)S(1)} %get-tuple-element.68), channel_id=1, source_target_pairs={{0,1},{1,0},{2,3},{3,2},{4,5},{5,4},{6,7},{7,6},{8,9},{9,8},{10,11... | collective-permute-start | bytes 182792 | tf_op jit(solution)/shard_map/ppermute | solution.py:26
  67.1 2.3 %collective-permute-done.7 = bf16[7,34,1,128]{3,0,2,1:T(8,128)(2,1)S(1)} collective-permute-done((bf16[7,34,1,128]{3,0,2,1:T(8,128)(2,1)S(1)}, bf16[7,34,1,128]{3,0,2,1:T(8,128)(2,1)S(1)}, u32[]{:S(2)}, u32[]{:S(2)}) %collective-permute-start.7) | collective-permute-done | bytes 60960 | tf_op jit(solution)/shard_map/ppermute | solution.py:26
  70.6 1.3 %maximum_convert_fusion.1 = f32[7,34,34,128]{3,0,2,1:T(8,128)S(1)} fusion(bf16[7,34,1,128]{3,0,2,1:T(8,128)(2,1)S(1)} %collective-permute-done.8, bf16[7,1,32,128]{3,0,2,1:T(8,128)(2,1)S(1)} %collective-permute-done.6, bf16[7,32,32,128]{3,0,2,1:T(8,128)(2,1)S(1)} %get-tuple-element.54, bf16[7,1,32,128]{3,0,2,1:T(8,128)(2,1)S(1)} %collective-permute-done.5, ...), kind=kLoop, calls=%fused_computation.33 | loop fusion | flops 5178880 | bytes 6214656 | tf_op jit(solution)/shard_map/convert_element_type | solution.py:100
  72.0 1.2 %fusion.19 = f32[1,34,34,128]{3,0,2,1:T(1,128)S(1)} fusion(f32[7,34,34,128]{3,0,2,1:T(8,128)S(1)} %fusion.34), kind=kLoop, calls=%fused_computation.36 | loop fusion | flops 147968 | bytes 1183744 | tf_op jit(solution)/shard_map/exp | solution.py:35
  75.5 3.5 %fusion.49 = (f32[7,32,32,1]{3,0,2,1:T(8,128)S(1)}, f32[7,32,32,1]{3,0,2,1:T(8,128)}) fusion(f32[7,34,34,128]{3,0,2,1:T(8,128)S(1)} %fusion.34), kind=kLoop, calls=%fused_computation.108 | loop fusion | bytes 114688 | tf_op jit(solution)/shard_map/jit(_roll_static)/slice | solution.py:46
  79.0 4.8 %fusion.48 = (f32[7,32,32,127]{3,0,2,1:T(8,128)}, f32[7,32,32,127]{3,0,2,1:T(8,128)}) fusion(f32[7,34,34,128]{3,0,2,1:T(8,128)S(1)} %fusion.34), kind=kLoop, calls=%fused_computation.107 | loop fusion | bytes 14565376 | tf_op jit(solution)/shard_map/jit(_roll_static)/slice | solution.py:46
  83.9 5.0 %fusion.25 = (f32[1,32,32,128]{3,0,2,1:T(1,128)S(1)}, f32[1,32,32,128]{3,0,2,1:T(1,128)S(1)}, f32[1,32,32,128]{3,0,2,1:T(1,128)S(1)}, f32[1,32,32,128]{3,0,2,1:T...) fusion(f32[1,34,34,128]{3,0,2,1:T(1,128)S(1)} %fusion.19, f32[1,32,32,127]{3,0,2,1:T(1,128)S(1)} %get-tuple-element.84, ...), kind=kLoop, calls=%fused_computation.47 | loop fusion | flops 1835008 | bytes 6815744 | tf_op jit(solution)/shard_map/mul | solution.py:50
  88.8 12.1 %fusion.17 = f32[1,7,32,32,128]{4,1,3,2,0:T(8,128)S(1)} fusion(f32[1,7,32,32,128]{4,3,2,1,0:T(8,128)S(1)} %copy-done, f32[7,32,32,128]{3,0,2,1:T(8,128)S(1)} %get-tuple-element.55, f32[7,32,32,127]{3,0,2,1:T(8,128)} %get-tuple-element.61, f32[7,32,32,1]{3,0,2,1:T(8,128)} %get-tuple-element.63, f32[7,32,32,1]{3,0,2,1:T(8,128)S(1)} %get-tuple-element.62, ...), kind=kLoop, calls=%fused_computation.31 | loop fusion | flops 25690112 | bytes 39977044 | tf_op jit(solution)/shard_map/broadcast_in_dim | solution.py:106
  100.9 2.5 %copy.21 = f32[1,7,32,32,128]{4,3,2,1,0:T(8,128)} copy(f32[1,7,32,32,128]{4,1,3,2,0:T(8,128)S(1)} %fusion.17) | data formatting | bytes 7340032 | tf_op jit(solution)/shard_map/broadcast_in_dim | solution.py:106
  (57 shorter events, 11.6 us)
Async XLA Ops:
  0.0 11.3 %copy-start.6 = (u32[32]{0:T(128)S(1)}, u32[32]{0:T(128)}, u32[]{:S(2)}) copy-start(u32[32]{0:T(128)} %constant.162) | copy-start | bytes 388
  0.0 12.5 %copy-start.5 = (s32[32]{0:T(128)S(1)}, s32[32]{0:T(128)}, u32[]{:S(2)}) copy-start(s32[32]{0:T(128)} %param.19) | copy-start | bytes 388
  0.0 18.0 %copy-start.3 = (f32[2,7]{1,0:T(2,128)S(1)}, f32[2,7]{1,0:T(2,128)}, u32[]{:S(2)}) copy-start(f32[2,7]{1,0:T(2,128)} %param.16) | copy-start | bytes 172
  0.0 18.0 %copy-start.2 = (s32[32,32,128]{2,1,0:T(8,128)S(1)}, s32[32,32,128]{2,1,0:T(8,128)}, u32[]{:S(2)}) copy-start(s32[32,32,128]{2,1,0:T(8,128)} %param.18) | copy-start | bytes 1572868
  0.0 18.1 %copy-start.4 = (f32[2,7]{1,0:T(2,128)S(1)}, f32[2,7]{1,0:T(2,128)}, u32[]{:S(2)}) copy-start(f32[2,7]{1,0:T(2,128)} %param.17) | copy-start | bytes 172
  5.4 12.7 %collective-permute-start.4 = (bf16[7,32,128]{2,0,1:T(8,128)(2,1)S(1)}, bf16[7,32,128]{2,0,1:T(8,128)(2,1)S(1)}, u32[]{:S(2)}, u32[]{:S(2)}) collective-permute-start(bf16[7,32,128]{2,0,1:T(8,128)(2,1)S(1)} %get-tuple-element.74), channel_id=1, source_target_pairs={{0,16},{16,0},{1,17},{17,1},{2,18},{18,2},{3,19},{19,3},{4,20},{20... | collective-permute-start | bytes 172040 | tf_op jit(solution)/shard_map/ppermute | solution.py:17
  8.5 15.4 %collective-permute-start.1 = (bf16[7,1,32,128]{3,0,2,1:T(8,128)(2,1)S(1)}, bf16[7,1,32,128]{3,0,2,1:T(8,128)(2,1)S(1)}, u32[]{:S(2)}, u32[]{:S(2)}) collective-permute-start(bf16[7,1,32,128]{3,0,2,1:T(8,128)(2,1)S(1)} %get-tuple-element.75), channel_id=1, source_target_pairs={{2,0},{4,2},{6,4},{8,6},{10,8},{12,10},{14,12},{0,14},{3,1},{5,3},... | collective-permute-start | bytes 172040 | tf_op jit(solution)/shard_map/ppermute | solution.py:29
  11.2 12.6 %collective-permute-start = (bf16[7,1,32,128]{3,0,2,1:T(8,128)(2,1)S(1)}, bf16[7,1,32,128]{3,0,2,1:T(8,128)(2,1)S(1)}, u32[]{:S(2)}, u32[]{:S(2)}) collective-permute-start(bf16[7,1,32,128]{3,0,2,1:T(8,128)(2,1)S(1)} %get-tuple-element.76), channel_id=1, source_target_pairs={{0,2},{2,4},{4,6},{6,8},{8,10},{10,12},{12,14},{14,0},{1,3},{3,5},... | collective-permute-start | bytes 172040 | tf_op jit(solution)/shard_map/ppermute | solution.py:26
  18.1 29.4 %copy-start.1 = (pred[32,32,128]{2,1,0:T(8,128)(4,1)}, pred[32,32,128]{2,1,0:T(8,128)(4,1)S(1)}, u32[]{:S(2)}) copy-start(pred[32,32,128]{2,1,0:T(8,128)(4,1)S(1)} %compare_and_fusion) | copy-start | bytes 393220
  23.9 4.4 %collective-permute-start.2 = (bf16[7,34,1,128]{3,0,2,1:T(8,128)(2,1)S(1)}, bf16[7,34,1,128]{3,0,2,1:T(8,128)(2,1)S(1)}, u32[]{:S(2)}, u32[]{:S(2)}) collective-permute-start(bf16[7,34,1,128]{3,0,2,1:T(8,128)(2,1)S(1)} %get-tuple-element.70), channel_id=1, source_target_pairs={{0,1},{1,0},{2,3},{3,2},{4,5},{5,4},{6,7},{7,6},{8,9},{9,8},{10,11... | collective-permute-start | bytes 182792 | tf_op jit(solution)/shard_map/ppermute | solution.py:26
  25.5 4.3 %collective-permute-start.3 = (bf16[7,34,1,128]{3,0,2,1:T(8,128)(2,1)S(1)}, bf16[7,34,1,128]{3,0,2,1:T(8,128)(2,1)S(1)}, u32[]{:S(2)}, u32[]{:S(2)}) collective-permute-start(bf16[7,34,1,128]{3,0,2,1:T(8,128)(2,1)S(1)} %get-tuple-element.71), channel_id=1, source_target_pairs={{1,0},{0,1},{3,2},{2,3},{5,4},{4,5},{7,6},{6,7},{9,8},{8,9},{11,10... | collective-permute-start | bytes 182792 | tf_op jit(solution)/shard_map/ppermute | solution.py:29
  43.1 4.4 %copy-start = (f32[1,7,32,32,128]{4,3,2,1,0:T(8,128)S(1)}, f32[1,7,32,32,128]{4,3,2,1,0:T(8,128)}, u32[]{:S(2)}) copy-start(f32[1,7,32,32,128]{4,3,2,1,0:T(8,128)} %param.15) | copy-start | bytes 11010052
  59.3 5.7 %collective-permute-start.5 = (bf16[7,1,32,128]{3,0,2,1:T(8,128)(2,1)S(1)}, bf16[7,1,32,128]{3,0,2,1:T(8,128)(2,1)S(1)}, u32[]{:S(2)}, u32[]{:S(2)}) collective-permute-start(bf16[7,1,32,128]{3,0,2,1:T(8,128)(2,1)S(1)} %get-tuple-element.72), channel_id=1, source_target_pairs={{0,2},{2,4},{4,6},{6,8},{8,10},{10,12},{12,14},{14,0},{1,3},{3,5},... | collective-permute-start | bytes 172040 | tf_op jit(solution)/shard_map/ppermute | solution.py:26
  59.4 5.6 %collective-permute-start.6 = (bf16[7,1,32,128]{3,0,2,1:T(8,128)(2,1)S(1)}, bf16[7,1,32,128]{3,0,2,1:T(8,128)(2,1)S(1)}, u32[]{:S(2)}, u32[]{:S(2)}) collective-permute-start(bf16[7,1,32,128]{3,0,2,1:T(8,128)(2,1)S(1)} %get-tuple-element.73), channel_id=1, source_target_pairs={{2,0},{4,2},{6,4},{8,6},{10,8},{12,10},{14,12},{0,14},{3,1},{5,3},... | collective-permute-start | bytes 172040 | tf_op jit(solution)/shard_map/ppermute | solution.py:29
  65.1 4.4 %collective-permute-start.7 = (bf16[7,34,1,128]{3,0,2,1:T(8,128)(2,1)S(1)}, bf16[7,34,1,128]{3,0,2,1:T(8,128)(2,1)S(1)}, u32[]{:S(2)}, u32[]{:S(2)}) collective-permute-start(bf16[7,34,1,128]{3,0,2,1:T(8,128)(2,1)S(1)} %get-tuple-element.68), channel_id=1, source_target_pairs={{0,1},{1,0},{2,3},{3,2},{4,5},{5,4},{6,7},{7,6},{8,9},{9,8},{10,11... | collective-permute-start | bytes 182792 | tf_op jit(solution)/shard_map/ppermute | solution.py:26
  66.3 4.3 %collective-permute-start.8 = (bf16[7,34,1,128]{3,0,2,1:T(8,128)(2,1)S(1)}, bf16[7,34,1,128]{3,0,2,1:T(8,128)(2,1)S(1)}, u32[]{:S(2)}, u32[]{:S(2)}) collective-permute-start(bf16[7,34,1,128]{3,0,2,1:T(8,128)(2,1)S(1)} %get-tuple-element.69), channel_id=1, source_target_pairs={{1,0},{0,1},{3,2},{2,3},{5,4},{4,5},{7,6},{6,7},{9,8},{8,9},{11,10... | collective-permute-start | bytes 182792 | tf_op jit(solution)/shard_map/ppermute | solution.py:29
where the time goes:
time: 104 us; the launch traced here: 103 us
  other arithmetic  39.1 us (38%)
  local copies, waits for them, and re-layouts  31.9 us (31%)
  starting transfers between devices  13.6 us (13%)
  blocking collectives  9.9 us (10%)
  waiting for transfers between devices  7.89 us (8%)
    slice x4, local copies, waits for them, and re-layouts, rates(): upper = jnp.roll(mid, -1, 3)  16.7 us
    broadcast_in_dim x1, other arithmetic, body(): return result[None]  12.1 us
    convert_element_type x1, other arithmetic, with_rim(): block.astype(jnp.bfloat16)  11.8 us
    mul x2, other arithmetic, rates(): 0.5 * (gmid + geast) * (east - mid) - 0.5 * (gmid + gwest) * (mid - west)  9.4 us
    ppermute x4, starting transfers between devices, extended(): lax.ppermute(lax.slice_in_dim(block, 0, width, axis=dim), axis, backward)  7.71 us
    unnamed x18, local copies, waits for them, and re-layouts  6.24 us
    all_gather x1, blocking collectives, body(): lax.all_gather(across.astype(jnp.bfloat16), 'gy', axis=1, tiled=True)  5.65 us
    ppermute x4, waiting for transfers between devices, extended(): lax.ppermute(lax.slice_in_dim(block, block.shape[dim] - width, None, axis...  5.25 us
  transfers between devices with their start and end apart: 9, of which 5 were waited for; matrix products, arithmetic and copies ran while one was open for 3% of the time, Pallas kernels for 0%

commit v1 on v0

--- a/solution.py
+++ b/solution.py
@@ -5,6 +5,18 @@
 
 RATIO = 1.5
 GAIN = 0.4
+
+
+def collect(x, axis, dim):
+    ways, here = (lax.axis_size(axis), lax.axis_index(axis))
+    grown, reach = (x, 1)
+    while reach < ways:
+        theirs = lax.ppermute(grown, axis, [(d, d ^ reach) for d in range(ways)])
+        mine_first = jnp.concatenate([grown, theirs], axis=dim)
+        theirs_first = jnp.concatenate([theirs, grown], axis=dim)
+        grown = jnp.where(here & reach == 0, mine_first, theirs_first)
+        reach = 2 * reach
+    return grown
 
 
 def swapped(block, axis, apart):
@@ -86,9 +98,7 @@
     on_right = stream_pos == last_block
     solid = (solid_mask == 1) & turbine
     across = swapped(fields[:, 0].astype(jnp.bfloat16), "comp", 0).astype(jnp.float32)
-    interface = lax.all_gather(across.astype(jnp.bfloat16), "gy", axis=1, tiled=True).astype(
-        across.dtype
-    )
+    interface = collect(across.astype(jnp.bfloat16), "gy", 1).astype(across.dtype)
     map_whole = lax.all_gather(iface_map, "gy", axis=0, tiled=True)
     rows_dev = fields.shape[2]
     row_base = lax.axis_index("gy") * rows_dev

time: 104 us -> 98.9 us (0.951)
  blocking collectives: 9.9 us -> 4.25 us
  starting transfers between devices: 13.6 us -> 15.2 us
    all_gather x1 -> x0, blocking collectives: 5.65 us -> none  [body(): lax.all_gather(across.astype(jnp.bfloat16), 'gy', axis=1, tiled=True)]
    ppermute x0 -> x1, starting transfers between devices: none -> 1.57 us  [collect(): theirs = lax.ppermute(grown, axis, [(d, d ^ reach) for d in range(ways)])]
  transfers between devices with their start and end apart: 9 -> 10, of which waited for: 5 -> 6; matrix products, arithmetic and copies ran while one was open for 3% -> 3% of each run, Pallas kernels for 0% -> 0%
where the time goes in v1:
time: 98.9 us; the launch traced here: 98.7 us
  other arithmetic  39.1 us (40%)
  local copies, waits for them, and re-layouts  32 us (32%)
  starting transfers between devices  15.2 us (15%)
  waiting for transfers between devices  7.27 us (7%)
  blocking collectives  4.25 us (4%)
  between operations  1 us (1%)
    slice x4, local copies, waits for them, and re-layouts, rates(): upper = jnp.roll(mid, -1, 3)  16.7 us
    broadcast_in_dim x1, other arithmetic, body(): return result[None]  12.1 us
    convert_element_type x1, other arithmetic, with_rim(): block.astype(jnp.bfloat16)  11.8 us
    mul x2, other arithmetic, rates(): 0.5 * (gmid + geast) * (east - mid) - 0.5 * (gmid + gwest) * (mid - west)  9.41 us
    ppermute x4, starting transfers between devices, extended(): lax.ppermute(lax.slice_in_dim(block, 0, width, axis=dim), axis, backward)  8.53 us
    unnamed x18, local copies, waits for them, and re-layouts  6.24 us
    ppermute x4, waiting for transfers between devices, extended(): lax.ppermute(lax.slice_in_dim(block, block.shape[dim] - width, None, axis...  4.61 us
    slice x4, local copies, waits for them, and re-layouts, rates(): gupper = jnp.roll(gmid, -1, 3)  4.6 us
  transfers between devices with their start and end apart: 10, of which 6 were waited for; matrix products, arithmetic and copies ran while one was open for 3% of the time, Pallas kernels for 0%

profile of v1, /device:TPU:0, one launch (start us, length us, event | category | flops | bytes accessed | tf_op | source)
XLA Modules:
  0.0 98.7 jit_solution(3038288952328975110)
XLA Ops:
  0.0 5.4 %copy.24 = bf16[1,7,32,32,128]{4,1,3,2,0:T(8,128)(2,1)S(1)} copy(f32[1,7,32,32,128]{4,3,2,1,0:T(8,128)} %param.15) | data formatting | bytes 5505024 | tf_op args[0]
  5.4 3.0 %collective-permute-start.4 = (bf16[7,32,128]{2,0,1:T(8,128)(2,1)S(1)}, bf16[7,32,128]{2,0,1:T(8,128)(2,1)S(1)}, u32[]{:S(2)}, u32[]{:S(2)}) collective-permute-start(bf16[7,32,128]{2,0,1:T(8,128)(2,1)S(1)} %get-tuple-element.74), channel_id=1, source_target_pairs={{0,16},{16,0},{1,17},{17,1},{2,18},{18,2},{3,19},{19,3},{4,20},{20... | collective-permute-start | bytes 172040 | tf_op jit(solution)/shard_map/ppermute | solution.py:29
  8.5 2.8 %collective-permute-start.1 = (bf16[7,1,32,128]{3,0,2,1:T(8,128)(2,1)S(1)}, bf16[7,1,32,128]{3,0,2,1:T(8,128)(2,1)S(1)}, u32[]{:S(2)}, u32[]{:S(2)}) collective-permute-start(bf16[7,1,32,128]{3,0,2,1:T(8,128)(2,1)S(1)} %get-tuple-element.75), channel_id=1, source_target_pairs={{2,0},{4,2},{6,4},{8,6},{10,8},{12,10},{14,12},{0,14},{3,1},{5,3},... | collective-permute-start | bytes 172040 | tf_op jit(solution)/shard_map/ppermute | solution.py:41
  12.8 4.3 %all-reduce.1 = s32[64]{0:T(128)S(1)} all-reduce(s32[64]{0:T(128)S(1)} %dynamic-update-slice.12), channel_id=1, replica_groups=mesh['comp'=2,'gx'=8,'gy'=2] {'gy'}, use_global_device_ids=true, to_apply=%add.1 | all-reduce | flops 64 | bytes 512
  18.2 1.6 %collective-permute-start.5 = (bf16[7,32,128]{2,0,1:T(8,128)(2,1)S(1)}, bf16[7,32,128]{2,0,1:T(8,128)(2,1)S(1)}, u32[]{:S(2)}, u32[]{:S(2)}) collective-permute-start(bf16[7,32,128]{2,0,1:T(8,128)(2,1)S(1)} %collective-permute-done.4), channel_id=1, source_target_pairs={{0,1},{1,0},{2,3},{3,2},{4,5},{5,4},{6,7},{7,6},{8,9},{9,8},{10,11... | collective-permute-start | bytes 172040 | tf_op jit(solution)/shard_map/ppermute | solution.py:14
  20.4 1.5 %collective-permute-start.3 = (bf16[7,34,1,128]{3,0,2,1:T(8,128)(2,1)S(1)}, bf16[7,34,1,128]{3,0,2,1:T(8,128)(2,1)S(1)}, u32[]{:S(2)}, u32[]{:S(2)}) collective-permute-start(bf16[7,34,1,128]{3,0,2,1:T(8,128)(2,1)S(1)} %get-tuple-element.71), channel_id=1, source_target_pairs={{1,0},{0,1},{3,2},{2,3},{5,4},{4,5},{7,6},{6,7},{9,8},{8,9},{11,10... | collective-permute-start | bytes 182792 | tf_op jit(solution)/shard_map/ppermute | solution.py:41
  24.9 1.3 %maximum_convert_fusion = f32[7,34,34,128]{3,0,2,1:T(8,128)S(1)} fusion(bf16[7,34,1,128]{3,0,2,1:T(8,128)(2,1)S(1)} %collective-permute-done.3, bf16[7,1,32,128]{3,0,2,1:T(8,128)(2,1)S(1)} %collective-permute-done.1, bf16[7,32,32,128]{3,0,2,1:T(8,128)(2,1)S(1)} %bitcast.66, bf16[7,1,32,128]{3,0,2,1:T(8,128)(2,1)S(1)} %collective-permute-done, ...), kind=kLoop, calls=%fused_computation.32 | loop fusion | flops 5178880 | bytes 6214656 | tf_op jit(solution)/shard_map/convert_element_type | solution.py:110
  26.3 1.2 %fusion.21 = f32[1,34,34,128]{3,0,2,1:T(1,128)S(1)} fusion(f32[7,34,34,128]{3,0,2,1:T(8,128)S(1)} %fusion.38), kind=kLoop, calls=%fused_computation.39 | loop fusion | flops 147968 | bytes 1183744 | tf_op jit(solution)/shard_map/exp | solution.py:47
  29.9 3.5 %fusion.52 = (f32[7,32,32,1]{3,0,2,1:T(8,128)S(1)}, f32[7,32,32,1]{3,0,2,1:T(8,128)}) fusion(f32[7,34,34,128]{3,0,2,1:T(8,128)S(1)} %fusion.38), kind=kLoop, calls=%fused_computation.111 | loop fusion | bytes 114688 | tf_op jit(solution)/shard_map/jit(_roll_static)/slice | solution.py:58
  33.4 4.8 %fusion.51 = (f32[7,32,32,127]{3,0,2,1:T(8,128)}, f32[7,32,32,127]{3,0,2,1:T(8,128)}) fusion(f32[7,34,34,128]{3,0,2,1:T(8,128)S(1)} %fusion.38), kind=kLoop, calls=%fused_computation.110 | loop fusion | bytes 14565376 | tf_op jit(solution)/shard_map/jit(_roll_static)/slice | solution.py:58
  38.2 4.4 %fusion.29 = (f32[1,32,32,128]{3,0,2,1:T(1,128)S(1)}, f32[1,32,32,128]{3,0,2,1:T(1,128)S(1)}, f32[1,32,32,128]{3,0,2,1:T(1,128)S(1)}, f32[1,32,32,128]{3,0,2,1:T...) fusion(f32[1,34,34,128]{3,0,2,1:T(1,128)S(1)} %fusion.21, ...), kind=kLoop, calls=%fused_computation.55 | loop fusion | flops 1835008 | bytes 6815744 | tf_op jit(solution)/shard_map/mul | solution.py:62
  42.7 11.8 %fusion.47 = (bf16[7,32,32,128]{3,0,2,1:T(8,128)(2,1)S(1)}, f32[7,32,32,128]{3,0,2,1:T(8,128)S(1)}) fusion(f32[7]{0:T(128)S(1)} %fusion.43, f32[7]{0:T(128)S(1)} %get-tuple-element.57, f32[7,32,32,127]{3,0,2,1:T(8,128)} %get-tuple-element.65, f32[7,32,32,1]{3,0,2,1:T(8,128)} %get-tuple-element.67, f32[32,32,128]{2,1,0:T(8,128)S(1)} %bitcast.74, ...), kind=kLoop, calls=%fused_computation.107 | loop fusion | flops 24772608 | bytes 38142036 | tf_op jit(solution)/shard_map/convert_element_type | solution.py:110
  54.6 3.5 %collective-permute-start.7 = (bf16[7,1,32,128]{3,0,2,1:T(8,128)(2,1)S(1)}, bf16[7,1,32,128]{3,0,2,1:T(8,128)(2,1)S(1)}, u32[]{:S(2)}, u32[]{:S(2)}) collective-permute-start(bf16[7,1,32,128]{3,0,2,1:T(8,128)(2,1)S(1)} %get-tuple-element.73), channel_id=1, source_target_pairs={{2,0},{4,2},{6,4},{8,6},{10,8},{12,10},{14,12},{0,14},{3,1},{5,3},... | collective-permute-start | bytes 172040 | tf_op jit(solution)/shard_map/ppermute | solution.py:41
  58.1 2.0 %collective-permute-done.6 = bf16[7,1,32,128]{3,0,2,1:T(8,128)(2,1)S(1)} collective-permute-done((bf16[7,1,32,128]{3,0,2,1:T(8,128)(2,1)S(1)}, bf16[7,1,32,128]{3,0,2,1:T(8,128)(2,1)S(1)}, u32[]{:S(2)}, u32[]{:S(2)}) %collective-permute-start.6) | collective-permute-done | bytes 57376 | tf_op jit(solution)/shard_map/ppermute | solution.py:38
  60.2 1.4 %collective-permute-start.8 = (bf16[7,34,1,128]{3,0,2,1:T(8,128)(2,1)S(1)}, bf16[7,34,1,128]{3,0,2,1:T(8,128)(2,1)S(1)}, u32[]{:S(2)}, u32[]{:S(2)}) collective-permute-start(bf16[7,34,1,128]{3,0,2,1:T(8,128)(2,1)S(1)} %get-tuple-element.68), channel_id=1, source_target_pairs={{0,1},{1,0},{2,3},{3,2},{4,5},{5,4},{6,7},{7,6},{8,9},{9,8},{10,11... | collective-permute-start | bytes 182792 | tf_op jit(solution)/shard_map/ppermute | solution.py:38
  62.3 2.3 %collective-permute-done.8 = bf16[7,34,1,128]{3,0,2,1:T(8,128)(2,1)S(1)} collective-permute-done((bf16[7,34,1,128]{3,0,2,1:T(8,128)(2,1)S(1)}, bf16[7,34,1,128]{3,0,2,1:T(8,128)(2,1)S(1)}, u32[]{:S(2)}, u32[]{:S(2)}) %collective-permute-start.8) | collective-permute-done | bytes 60960 | tf_op jit(solution)/shard_map/ppermute | solution.py:38
  64.6 1.3 %collective-permute-done.9 = bf16[7,34,1,128]{3,0,2,1:T(8,128)(2,1)S(1)} collective-permute-done((bf16[7,34,1,128]{3,0,2,1:T(8,128)(2,1)S(1)}, bf16[7,34,1,128]{3,0,2,1:T(8,128)(2,1)S(1)}, u32[]{:S(2)}, u32[]{:S(2)}) %collective-permute-start.9) | collective-permute-done | bytes 60960 | tf_op jit(solution)/shard_map/ppermute | solution.py:41
  65.8 1.3 %maximum_convert_fusion.1 = f32[7,34,34,128]{3,0,2,1:T(8,128)S(1)} fusion(bf16[7,34,1,128]{3,0,2,1:T(8,128)(2,1)S(1)} %collective-permute-done.9, bf16[7,1,32,128]{3,0,2,1:T(8,128)(2,1)S(1)} %collective-permute-done.7, bf16[7,32,32,128]{3,0,2,1:T(8,128)(2,1)S(1)} %get-tuple-element.54, bf16[7,1,32,128]{3,0,2,1:T(8,128)(2,1)S(1)} %collective-permute-done.6, ...), kind=kLoop, calls=%fused_computation.33 | loop fusion | flops 5178880 | bytes 6214656 | tf_op jit(solution)/shard_map/convert_element_type | solution.py:110
  67.2 1.2 %fusion.19 = f32[1,34,34,128]{3,0,2,1:T(1,128)S(1)} fusion(f32[7,34,34,128]{3,0,2,1:T(8,128)S(1)} %fusion.34), kind=kLoop, calls=%fused_computation.36 | loop fusion | flops 147968 | bytes 1183744 | tf_op jit(solution)/shard_map/exp | solution.py:47
  70.8 3.5 %fusion.50 = (f32[7,32,32,1]{3,0,2,1:T(8,128)S(1)}, f32[7,32,32,1]{3,0,2,1:T(8,128)}) fusion(f32[7,34,34,128]{3,0,2,1:T(8,128)S(1)} %fusion.34), kind=kLoop, calls=%fused_computation.109 | loop fusion | bytes 114688 | tf_op jit(solution)/shard_map/jit(_roll_static)/slice | solution.py:58
  74.3 4.8 %fusion.49 = (f32[7,32,32,127]{3,0,2,1:T(8,128)}, f32[7,32,32,127]{3,0,2,1:T(8,128)}) fusion(f32[7,34,34,128]{3,0,2,1:T(8,128)S(1)} %fusion.34), kind=kLoop, calls=%fused_computation.108 | loop fusion | bytes 14565376 | tf_op jit(solution)/shard_map/jit(_roll_static)/slice | solution.py:58
  79.2 5.0 %fusion.25 = (f32[1,32,32,128]{3,0,2,1:T(1,128)S(1)}, f32[1,32,32,128]{3,0,2,1:T(1,128)S(1)}, f32[1,32,32,128]{3,0,2,1:T(1,128)S(1)}, f32[1,32,32,128]{3,0,2,1:T...) fusion(f32[1,34,34,128]{3,0,2,1:T(1,128)S(1)} %fusion.19, f32[1,32,32,127]{3,0,2,1:T(1,128)S(1)} %get-tuple-element.84, ...), kind=kLoop, calls=%fused_computation.47 | loop fusion | flops 1835008 | bytes 6815744 | tf_op jit(solution)/shard_map/mul | solution.py:62
  84.2 12.1 %fusion.17 = f32[1,7,32,32,128]{4,1,3,2,0:T(8,128)S(1)} fusion(f32[1,7,32,32,128]{4,3,2,1,0:T(8,128)S(1)} %copy-done, f32[7,32,32,128]{3,0,2,1:T(8,128)S(1)} %get-tuple-element.55, f32[7,32,32,127]{3,0,2,1:T(8,128)} %get-tuple-element.61, f32[7,32,32,1]{3,0,2,1:T(8,128)} %get-tuple-element.63, f32[7,32,32,1]{3,0,2,1:T(8,128)S(1)} %get-tuple-element.62, ...), kind=kLoop, calls=%fused_computation.31 | loop fusion | flops 25690112 | bytes 39977044 | tf_op jit(solution)/shard_map/broadcast_in_dim | solution.py:116
  96.2 2.5 %copy.15 = f32[1,7,32,32,128]{4,3,2,1,0:T(8,128)} copy(f32[1,7,32,32,128]{4,1,3,2,0:T(8,128)S(1)} %fusion.17) | data formatting | bytes 7340032 | tf_op jit(solution)/shard_map/broadcast_in_dim | solution.py:116
  (57 shorter events, 11.1 us)
Async XLA Ops:
  0.0 11.3 %copy-start.6 = (u32[32]{0:T(128)S(1)}, u32[32]{0:T(128)}, u32[]{:S(2)}) copy-start(u32[32]{0:T(128)} %constant.162) | copy-start | bytes 388
  0.0 12.5 %copy-start.5 = (s32[32]{0:T(128)S(1)}, s32[32]{0:T(128)}, u32[]{:S(2)}) copy-start(s32[32]{0:T(128)} %param.19) | copy-start | bytes 388
  0.0 18.0 %copy-start.3 = (f32[2,7]{1,0:T(2,128)S(1)}, f32[2,7]{1,0:T(2,128)}, u32[]{:S(2)}) copy-start(f32[2,7]{1,0:T(2,128)} %param.16) | copy-start | bytes 172
  0.0 18.0 %copy-start.2 = (s32[32,32,128]{2,1,0:T(8,128)S(1)}, s32[32,32,128]{2,1,0:T(8,128)}, u32[]{:S(2)}) copy-start(s32[32,32,128]{2,1,0:T(8,128)} %param.18) | copy-start | bytes 1572868
  0.0 18.1 %copy-start.4 = (f32[2,7]{1,0:T(2,128)S(1)}, f32[2,7]{1,0:T(2,128)}, u32[]{:S(2)}) copy-start(f32[2,7]{1,0:T(2,128)} %param.17) | copy-start | bytes 172
  5.4 12.7 %collective-permute-start.4 = (bf16[7,32,128]{2,0,1:T(8,128)(2,1)S(1)}, bf16[7,32,128]{2,0,1:T(8,128)(2,1)S(1)}, u32[]{:S(2)}, u32[]{:S(2)}) collective-permute-start(bf16[7,32,128]{2,0,1:T(8,128)(2,1)S(1)} %get-tuple-element.74), channel_id=1, source_target_pairs={{0,16},{16,0},{1,17},{17,1},{2,18},{18,2},{3,19},{19,3},{4,20},{20... | collective-permute-start | bytes 172040 | tf_op jit(solution)/shard_map/ppermute | solution.py:29
  8.5 11.3 %collective-permute-start.1 = (bf16[7,1,32,128]{3,0,2,1:T(8,128)(2,1)S(1)}, bf16[7,1,32,128]{3,0,2,1:T(8,128)(2,1)S(1)}, u32[]{:S(2)}, u32[]{:S(2)}) collective-permute-start(bf16[7,1,32,128]{3,0,2,1:T(8,128)(2,1)S(1)} %get-tuple-element.75), channel_id=1, source_target_pairs={{2,0},{4,2},{6,4},{8,6},{10,8},{12,10},{14,12},{0,14},{3,1},{5,3},... | collective-permute-start | bytes 172040 | tf_op jit(solution)/shard_map/ppermute | solution.py:41
  11.2 8.5 %collective-permute-start = (bf16[7,1,32,128]{3,0,2,1:T(8,128)(2,1)S(1)}, bf16[7,1,32,128]{3,0,2,1:T(8,128)(2,1)S(1)}, u32[]{:S(2)}, u32[]{:S(2)}) collective-permute-start(bf16[7,1,32,128]{3,0,2,1:T(8,128)(2,1)S(1)} %get-tuple-element.76), channel_id=1, source_target_pairs={{0,2},{2,4},{4,6},{6,8},{8,10},{10,12},{12,14},{14,0},{1,3},{3,5},... | collective-permute-start | bytes 172040 | tf_op jit(solution)/shard_map/ppermute | solution.py:38
  18.1 24.5 %copy-start.1 = (pred[32,32,128]{2,1,0:T(8,128)(4,1)}, pred[32,32,128]{2,1,0:T(8,128)(4,1)S(1)}, u32[]{:S(2)}) copy-start(pred[32,32,128]{2,1,0:T(8,128)(4,1)S(1)} %compare_and_fusion) | copy-start | bytes 393220
  18.2 4.3 %collective-permute-start.5 = (bf16[7,32,128]{2,0,1:T(8,128)(2,1)S(1)}, bf16[7,32,128]{2,0,1:T(8,128)(2,1)S(1)}, u32[]{:S(2)}, u32[]{:S(2)}) collective-permute-start(bf16[7,32,128]{2,0,1:T(8,128)(2,1)S(1)} %collective-permute-done.4), channel_id=1, source_target_pairs={{0,1},{1,0},{2,3},{3,2},{4,5},{5,4},{6,7},{7,6},{8,9},{9,8},{10,11... | collective-permute-start | bytes 172040 | tf_op jit(solution)/shard_map/ppermute | solution.py:14
  19.8 4.4 %collective-permute-start.2 = (bf16[7,34,1,128]{3,0,2,1:T(8,128)(2,1)S(1)}, bf16[7,34,1,128]{3,0,2,1:T(8,128)(2,1)S(1)}, u32[]{:S(2)}, u32[]{:S(2)}) collective-permute-start(bf16[7,34,1,128]{3,0,2,1:T(8,128)(2,1)S(1)} %get-tuple-element.70), channel_id=1, source_target_pairs={{0,1},{1,0},{2,3},{3,2},{4,5},{5,4},{6,7},{7,6},{8,9},{9,8},{10,11... | collective-permute-start | bytes 182792 | tf_op jit(solution)/shard_map/ppermute | solution.py:38
  20.4 4.5 %collective-permute-start.3 = (bf16[7,34,1,128]{3,0,2,1:T(8,128)(2,1)S(1)}, bf16[7,34,1,128]{3,0,2,1:T(8,128)(2,1)S(1)}, u32[]{:S(2)}, u32[]{:S(2)}) collective-permute-start(bf16[7,34,1,128]{3,0,2,1:T(8,128)(2,1)S(1)} %get-tuple-element.71), channel_id=1, source_target_pairs={{1,0},{0,1},{3,2},{2,3},{5,4},{4,5},{7,6},{6,7},{9,8},{8,9},{11,10... | collective-permute-start | bytes 182792 | tf_op jit(solution)/shard_map/ppermute | solution.py:41
  38.2 4.4 %copy-start = (f32[1,7,32,32,128]{4,3,2,1,0:T(8,128)S(1)}, f32[1,7,32,32,128]{4,3,2,1,0:T(8,128)}, u32[]{:S(2)}) copy-start(f32[1,7,32,32,128]{4,3,2,1,0:T(8,128)} %param.15) | copy-start | bytes 11010052
  54.5 5.6 %collective-permute-start.6 = (bf16[7,1,32,128]{3,0,2,1:T(8,128)(2,1)S(1)}, bf16[7,1,32,128]{3,0,2,1:T(8,128)(2,1)S(1)}, u32[]{:S(2)}, u32[]{:S(2)}) collective-permute-start(bf16[7,1,32,128]{3,0,2,1:T(8,128)(2,1)S(1)} %get-tuple-element.72), channel_id=1, source_target_pairs={{0,2},{2,4},{4,6},{6,8},{8,10},{10,12},{12,14},{14,0},{1,3},{3,5},... | collective-permute-start | bytes 172040 | tf_op jit(solution)/shard_map/ppermute | solution.py:38
  54.6 5.6 %collective-permute-start.7 = (bf16[7,1,32,128]{3,0,2,1:T(8,128)(2,1)S(1)}, bf16[7,1,32,128]{3,0,2,1:T(8,128)(2,1)S(1)}, u32[]{:S(2)}, u32[]{:S(2)}) collective-permute-start(bf16[7,1,32,128]{3,0,2,1:T(8,128)(2,1)S(1)} %get-tuple-element.73), channel_id=1, source_target_pairs={{2,0},{4,2},{6,4},{8,6},{10,8},{12,10},{14,12},{0,14},{3,1},{5,3},... | collective-permute-start | bytes 172040 | tf_op jit(solution)/shard_map/ppermute | solution.py:41
  60.2 4.4 %collective-permute-start.8 = (bf16[7,34,1,128]{3,0,2,1:T(8,128)(2,1)S(1)}, bf16[7,34,1,128]{3,0,2,1:T(8,128)(2,1)S(1)}, u32[]{:S(2)}, u32[]{:S(2)}) collective-permute-start(bf16[7,34,1,128]{3,0,2,1:T(8,128)(2,1)S(1)} %get-tuple-element.68), channel_id=1, source_target_pairs={{0,1},{1,0},{2,3},{3,2},{4,5},{5,4},{6,7},{7,6},{8,9},{9,8},{10,11... | collective-permute-start | bytes 182792 | tf_op jit(solution)/shard_map/ppermute | solution.py:38
  61.5 4.3 %collective-permute-start.9 = (bf16[7,34,1,128]{3,0,2,1:T(8,128)(2,1)S(1)}, bf16[7,34,1,128]{3,0,2,1:T(8,128)(2,1)S(1)}, u32[]{:S(2)}, u32[]{:S(2)}) collective-permute-start(bf16[7,34,1,128]{3,0,2,1:T(8,128)(2,1)S(1)} %get-tuple-element.69), channel_id=1, source_target_pairs={{1,0},{0,1},{3,2},{2,3},{5,4},{4,5},{7,6},{6,7},{9,8},{8,9},{11,10... | collective-permute-start | bytes 182792 | tf_op jit(solution)/shard_map/ppermute | solution.py:41
